TPU v7x, 32 devices: a whole 2x2x4 slice. The times are simulated.
32 devices in a mesh: grp: 2 (over y), wide: 8 (over z, x), narrow: 2 (over core).
Axes of the slice: x: 2, y: 2, z: 4, core: 2. Of those that a mesh axis runs over, the one named last changes fastest.
Arguments:
- node_latent: bfloat16 [5120, 512], P(('grp', 'wide', 'narrow')), parts along dimension 0, may hold values from -6 to 6
- fine_edges: bfloat16 [30720, 512], P(('grp', 'wide', 'narrow')), parts along dimension 0, may hold values from -6 to 6
- fine_senders: int32 [30720], P(('grp', 'wide', 'narrow')), parts along dimension 0, may hold values from 0 to 2559, as said below
- fine_receivers: int32 [30720], P(('grp', 'wide', 'narrow')), parts along dimension 0, may hold values from 0 to 2559, as said below
- coarse_edges: bfloat16 [1024, 512], P(('grp', 'wide', 'narrow')), parts along dimension 0, may hold values from -6 to 6
- coarse_senders: int32 [1024], P(('grp', 'wide', 'narrow')), parts along dimension 0, may hold values from 0 to 2403, as said below
- coarse_receivers: int32 [1024], P(('grp', 'wide', 'narrow')), parts along dimension 0, may hold values from 0 to 2403, as said below
- edge_weight_in: bfloat16 [1536, 512], replicated, may hold values from -0.15625 to 0.15625
- edge_bias: float32 [512], replicated, may hold values from -3 to 3
- edge_weight_out: bfloat16 [512, 512], replicated, may hold values from -0.25 to 0.25
- edge_gain: float32 [512], replicated, may hold values from 0.5 to 1.5
- edge_shift: float32 [512], replicated, may hold values from -2 to 2
- node_weight_in: bfloat16 [1024, 512], replicated, may hold values from -0.1875 to 0.1875
- node_bias: float32 [512], replicated, may hold values from -3 to 3
- node_weight_out: bfloat16 [512, 512], replicated, may hold values from -0.25 to 0.25
- node_gain: float32 [512], replicated, may hold values from 0.5 to 1.5
- node_shift: float32 [512], replicated, may hold values from -2 to 2
Outputs:
- node_out: bfloat16 [5120, 512], P(('grp', 'wide', 'narrow')), parts along dimension 0
There are 2 independent parts, one for each index of `grp`. A program takes and returns all parts, laid end to end along the dimension named above; an argument that names none is the same for every part. Nothing has to cross between parts.
Inputs may be any that keep to these rules, and one draw needn't show every extreme that they name: `fine_receivers`: node v belongs to device v // 160 (devices numbered wide index times 2 plus narrow index) and to patch v // 320. Each block of 960 fine edges belongs to one device, in order, and its receivers are that device's nodes. `fine_senders`: the sender of a fine edge lies in the receiver's patch p, or is a boundary node (v % 160 >= 140) of a device of patch p - 1 or p + 1, modulo 8. `coarse_receivers`: coarse nodes are the nodes v with v % 160 < 4. Each block of 32 coarse edges belongs to one device, in order, and its receivers are that device's coarse nodes; each coarse node receives at least one. `coarse_senders`: every coarse sender is a coarse node, on any device.
All inputs are finite; a program needn't handle non-finite values.
Results may differ from a plain program's by a relative error of at most 0.0053.
Values may be sent and summed in bfloat16 or wider, within the bound.
No kernel may reach another device: no remote copies, remote signals or barrier semaphores. Data moves between devices by JAX's collectives and lax.ppermute only.
A program may use at most 64 MiB of HBM per device.

v0:
```python
import functools

import jax
import jax.numpy as jnp
from jax import lax
from jax.experimental import pallas as pl
from jax.experimental.pallas import tpu as pltpu
from jax.sharding import PartitionSpec as P


COARSE_DEV = 4
LANES = 128
CHUNKS = 3
LATE = 128
RING = 8
BF16 = jnp.bfloat16
F32 = jnp.float32
MIB = 1 << 20


def silu_of_half(u):
    return u + u * jnp.tanh(u)


def normalized(values):
    center = values - jnp.mean(values, axis=-1, keepdims=True)
    spread = jnp.mean(center * center, axis=-1, keepdims=True)
    return center * lax.rsqrt(spread + 1e-05)


def dot(a, b):
    return jnp.dot(a, b, preferred_element_type=F32)


def columns(row):
    return jnp.broadcast_to(row, (LANES, row.shape[1])).T


def one_hot(cols, width, value=1.0):
    lane = lax.broadcasted_iota(jnp.int32, cols[0].shape, 1)
    blocks = []
    for b in range(width // LANES):
        hit = cols[0] == lane + b * LANES
        for c in cols[1:]:
            hit = hit | (c == lane + b * LANES)
        blocks.append(jnp.where(hit, value, 0.0).astype(BF16))
    return jnp.concatenate(blocks, axis=1)


def stage_kernel(n, *refs):
    sems = refs[-1]
    copies = [pltpu.make_async_copy(refs[k], refs[k - n - 1], sems.at[k]) for k in range(n)]
    for c in copies:
        c.start()
    for c in copies:
        c.wait()


def pay_kernel(halo, nl, partner, pay):
    nodes = nl.shape[0]
    pick = lambda r: jnp.concatenate([r[nodes - halo :, :], r[:COARSE_DEV, :]], axis=0)
    own, other = pick(nl), pick(partner)
    low = lax.axis_index("narrow") == 0
    pay[...] = jnp.concatenate([jnp.where(low, own, other), jnp.where(low, other, own)], axis=0)


def coarse_of(rows, halo):
    block = halo + COARSE_DEV
    return [rows[halo:block, :], rows[block + halo : 2 * block, :]]


def pair_kernel(halo, pay, x_rows, _, known, rich):
    known[...] = jnp.concatenate(coarse_of(pay, halo) + coarse_of(x_rows, halo), axis=0)
    rich[...] = jnp.concatenate([known[...]] + halos_of(x_rows, halo), axis=0)


def both_kernel(first, second, _, __, both):
    n = first.shape[0]
    both[:n, :] = first[...]
    both[n:, :] = second[...]


def halos_of(rows, halo):
    block = halo + COARSE_DEV
    return [rows[:halo, :], rows[block : block + halo, :]]


def collect_kernel(halo, known, both, other, far, picks):
    n, m = 2 * halo, known.shape[0]
    low = lax.axis_index("narrow") == 0
    even = lax.axis_index("wide") % 2 == 0
    zero, one = jnp.where(low, both[...], other[...]), jnp.where(low, other[...], both[...])
    picks[...] = jnp.concatenate([known[...], one[:m], one[m + n :], zero[:m]], axis=0)
    source = jnp.where(even, zero[m : m + n], one[m : m + n])
    far[...] = jnp.concatenate([source, known[: 2 * COARSE_DEV]], axis=0)


def wrap_kernel(halo, y_rows, far):
    far[...] = jnp.concatenate(
        halos_of(y_rows[...], halo) + [y_rows[: 2 * COARSE_DEV, :]], axis=0
    )


def join_kernel(*refs):
    at = 0
    for r in refs[:-1]:
        refs[-1][at : at + r.shape[0], :] = r[...]
        at += r.shape[0]


def places(n_patches):
    wide = lax.axis_index("wide")
    half = lax.axis_index("narrow")
    y_patch = jnp.where(wide % 2 == 0, wide + n_patches - 1, wide + 1) % n_patches
    return wide, half, wide * 2 + half, y_patch


def local_kernel(
    nodes, halo, n_patches,
    nl, fs, fr, cs, cr, e_bias, n_bias, e_shift, ce, w_in, u_in,
    base_c, oh1, oh2, sel, inc_f, inc_e, inc_l, pack, late, shifts, nu, table,
):
    d = nl.shape[1]
    wide, half, device, y_patch = places(n_patches)
    patch = 2 * nodes
    first = nodes - halo
    block = halo + COARSE_DEV

    recv = fr[...] - device * nodes
    send = fs[...]

    def offset(p):
        off = send - p * patch
        inside = (off >= 0) & (off < patch)
        upper = (off >= nodes).astype(jnp.int32)
        return inside, upper, off - upper * nodes

    inside, upper, loc = offset(wide)
    own = jnp.where(inside & (upper == half), loc + nodes, -1)
    pos = jnp.where(inside & (upper != half), loc, -1)
    for k, p in enumerate((wide ^ 1, y_patch)):
        inside, upper, loc = offset(p)
        at = nodes + k * 2 * block + upper * (block, halo)[k] + loc - first
        pos = jnp.where(inside, at, pos)

    recv_c = cr[...] - device * nodes
    chip_rows = cs[...].astype(F32)
    owner = jnp.floor((chip_rows + 0.5) * (1.0 / nodes)).astype(jnp.int32)
    slot_c = cs[...] - owner * nodes
    patch_c = owner // 2
    if n_patches == RING:
        pairs = n_patches // 2
        place_c = (patch_c // 2 - wide // 2 + pairs) % pairs * 2 + (patch_c ^ wide) % 2
    else:
        place_c = patch_c ^ wide
    pos_c = place_c * (2 * COARSE_DEV) + (owner % 2) * COARSE_DEV + slot_c

    def incidence(ids):
        at = lax.broadcasted_iota(jnp.int32, (nodes, ids.shape[1]), 0)
        return jnp.where(at == ids, 1.0, 0.0)

    edges = fr.shape[1]
    last_block = pos >= nodes + 2 * block
    late_row = jnp.where(last_block, 1.0, 0.0)
    before = lax.broadcasted_iota(jnp.int32, (edges, edges), 0)
    before = before < lax.broadcasted_iota(jnp.int32, (edges, edges), 1)
    flags = jnp.broadcast_to(late_row, (8, edges)).astype(BF16)
    rank = dot(flags, jnp.where(before, 1.0, 0.0).astype(BF16))[0:1, :].astype(jnp.int32)
    rank = jnp.where(last_block, rank, -1)
    chosen = lax.broadcasted_iota(jnp.int32, pack.shape, 0) == rank
    chosen = jnp.where(chosen, 1.0, 0.0).astype(BF16)
    pack[...] = chosen
    over = jnp.sum(late_row, axis=1, keepdims=True) > LATE
    late[...] = jnp.broadcast_to(jnp.where(over, 1.0, 0.0), late.shape)
    marks, marks_c = incidence(recv), incidence(recv_c)
    inc_f[...] = marks.astype(BF16)
    inc_e[...] = (marks * (1.0 - late_row)).astype(BF16)
    inc_l[:, :LATE] = lax.dot_general(
        marks.astype(BF16), chosen, (((1,), (1,)), ((), ())), preferred_element_type=F32
    ).astype(BF16)
    inc_l[:, LATE:] = marks_c.astype(BF16)
    count = jnp.sum(marks, axis=1, keepdims=True) + jnp.sum(marks_c, axis=1, keepdims=True)
    shifts[...] = count * e_shift[...]
    wide_c = -(-sel.shape[1] // LANES) * LANES
    sel[...] = one_hot((columns(pos_c),), wide_c, 0.5)[:, : sel.shape[1]]
    oh_c = one_hot((columns(recv_c),), table.shape[0])
    oh1[...] = one_hot((columns(recv), columns(own)), oh1.shape[1], 0.5)
    oh2[...] = one_hot((columns(pos),), oh2.shape[1], 0.5)
    table[2 * nodes :, :] = jnp.zeros_like(table[2 * nodes :, :])

    node_rows = nl[...]
    table[0:nodes, :] = dot(node_rows, w_in[2 * d :, :]).astype(BF16)
    table[nodes : 2 * nodes, :] = dot(node_rows, w_in[d : 2 * d, :]).astype(BF16)
    nu[...] = 0.5 * (dot(node_rows, u_in[:d, :]) + n_bias[...])
    base_c[...] = 0.5 * (dot(ce[...], w_in[:d, :]) + dot(oh_c, table[...]) + e_bias[...])


def base_kernel(oh1, table, w_in, e_bias, fe, _, __, base_f):
    d = fe.shape[1]
    own = 0.5 * (dot(fe[...], w_in[:d, :]) + e_bias[...])
    base_f[...] = own + dot(oh1[...], table[...])


def w_send(w_in):
    d = w_in.shape[1]
    return w_in[d : 2 * d, :]


def prep_kernel(partner, x_rows, base_f, base_c, oh2, sel, pack, w_in, ready, hidden, part, pick):
    n = partner.shape[0]
    m = n + x_rows.shape[0]
    ready[:n, :] = dot(partner[...], w_send(w_in)).astype(BF16)
    ready[n:m, :] = dot(x_rows[...], w_send(w_in)).astype(BF16)
    ready[m:, :] = jnp.zeros_like(ready[m:, :])
    half = base_f[...]
    hidden[...] = silu_of_half(half + dot(oh2[...], ready[...])).astype(BF16)
    coarse_bits = half.astype(BF16)
    fine_bits = (half - coarse_bits.astype(F32)).astype(BF16)
    late = pack.shape[0]
    part[:late, :] = dot(pack[...], coarse_bits) + dot(pack[...], fine_bits)
    part[late:, :] = base_c[...]
    pick[...] = jnp.zeros_like(pick)
    pick[:late, :LANES] = dot(pack[...], oh2[:, oh2.shape[1] - LANES :]).astype(BF16)
    pick[late:, LANES:] = sel[...]


def early_kernel(hidden, inc_e, w_out, total, mess):
    rows = hidden.shape[0]
    step = rows // CHUNKS
    for k in range(CHUNKS):
        s = slice(k * step, (k + 1) * step)
        mess[s, :] = normalized(dot(hidden[s, :], w_out[...])).astype(BF16)
    total[...] = dot(inc_e[...], mess[...])


def last_kernel(
    n_pieces, ready, far, nl, base_f, part, pick, oh2, inc_f, inc_l, late,
    total, shifts, nu, w_in, w_out, u_in, u_out, e_gain, n_gain, n_shift, *refs,
):
    pieces, (out, rows, table, hidden, mess, acc) = refs[:n_pieces], refs[n_pieces:]
    w_s = w_send(w_in)
    a = LANES - far.shape[0]
    rows[:a, :] = jnp.zeros_like(rows[:a, :])
    rows[a:LANES, :] = far[...]
    rows[LANES:, :] = jnp.concatenate([r[...] for r in pieces], axis=0)
    picked = dot(pick[...], rows[...]).astype(BF16)
    half = part[...] + dot(picked, w_s)
    some = normalized(dot(silu_of_half(half).astype(BF16), w_out[...])).astype(BF16)
    acc[...] = total[...] + dot(inc_l[...], some)

    @pl.when(late[0, 0] > 0)
    def _():
        a = ready.shape[0] - far.shape[0]
        table[:a, :] = ready[:a, :]
        table[a:, :] = dot(far[...], w_s).astype(BF16)
        step = base_f.shape[0] // CHUNKS
        for k in range(CHUNKS):
            s = slice(k * step, (k + 1) * step)
            hidden[s, :] = silu_of_half(base_f[s, :] + dot(oh2[s, :], table[...])).astype(BF16)
            mess[s, :] = normalized(dot(hidden[s, :], w_out[...])).astype(BF16)
        acc[...] = dot(inc_f[...], mess[...]) + dot(inc_l[:, LATE:], some[LATE:])

    summed = acc[...] * e_gain[...] + shifts[...]
    d = nl.shape[1]
    half = nu[...] + 0.5 * dot(summed.astype(BF16), u_in[d:, :])
    update = normalized(dot(silu_of_half(half).astype(BF16), u_out[...]))
    out[...] = (nl[...].astype(F32) + (update * n_gain[...] + n_shift[...])).astype(BF16)


NEAR = pl.BlockSpec(memory_space=pltpu.VMEM)
FAR = pl.BlockSpec(memory_space=pltpu.HBM)


def near(*arrays):
    return [pltpu.with_memory_space_constraint(a, pltpu.VMEM) for a in arrays]


def call(kernel, near_in, outs, far_in=(), scratch=(), limit=8, far_out=False, cost=None):
    outs = [(o.shape, o.dtype) if hasattr(o, "shape") else o for o in outs]
    kind = (lambda s, t: jax.ShapeDtypeStruct(s, t)) if far_out else (lambda s, t: pltpu.VMEM(s, t))
    return pl.pallas_call(
        kernel,
        out_shape=tuple(kind(*o) for o in outs),
        in_specs=[NEAR] * len(near_in) + [FAR] * len(far_in),
        out_specs=tuple([NEAR] * len(outs)),
        scratch_shapes=list(scratch),
        compiler_params=pltpu.CompilerParams(vmem_limit_bytes=limit * MIB),
        cost_estimate=pl.CostEstimate(flops=cost or 0, bytes_accessed=cost or 0, transcendentals=0),
    )(*near(*near_in), *[pltpu.with_memory_space_constraint(a, pltpu.HBM) for a in far_in])


def shards(
    node_latent, fine_edges, fine_senders, fine_receivers, coarse_edges, coarse_senders,
    coarse_receivers, edge_weight_in, edge_bias, edge_weight_out, edge_gain, edge_shift,
    node_weight_in, node_bias, node_weight_out, node_gain, node_shift,
):
    nodes, d = node_latent.shape
    halo = nodes // 8
    block = halo + COARSE_DEV
    n_patches = lax.axis_size("wide")
    edges, coarse_count = fine_edges.shape[0], coarse_edges.shape[0]
    small = [node_latent] + [
        v.reshape(1, -1)
        for v in (
            fine_senders, fine_receivers, coarse_senders, coarse_receivers, edge_bias, node_bias,
            edge_gain, edge_shift, node_gain, node_shift,
        )
    ]
    dma = pltpu.SemaphoreType.DMA

    partner = lax.ppermute(node_latent, "narrow", [(0, 1), (1, 0)])
    nl, fs, fr, cs, cr, e_bias, n_bias, e_gain, e_shift, n_gain, n_shift = call(
        functools.partial(stage_kernel, len(small)), (), small,
        far_in=small + [fine_edges, edge_weight_in, node_weight_in], scratch=[dma((len(small),))], limit=1
    )
    (pay,) = call(functools.partial(pay_kernel, halo), (nl, partner), [((2 * block, d), BF16)], limit=1)
    around = range(n_patches)
    table_a = -(-2 * nodes // LANES) * LANES
    table_b = nodes + 4 * block
    base_c, oh1, oh2, sel, inc_f, inc_e, inc_l, pack, late, shifts, nu, table = call(
        functools.partial(local_kernel, nodes, halo, n_patches),
        (nl, fs, fr, cs, cr, e_bias, n_bias, e_shift, coarse_edges, edge_weight_in, node_weight_in),
        [
            ((coarse_count, d), F32),
            ((edges, table_a), BF16),
            ((edges, table_b), BF16),
            ((coarse_count, 2 * n_patches * COARSE_DEV), BF16),
            ((nodes, edges), BF16),
            ((nodes, edges), BF16),
            ((nodes, LATE + coarse_count), BF16),
            ((LATE, edges), BF16),
            ((8, LANES), F32),
            ((nodes, d), F32),
            ((nodes, d), F32),
            ((table_a, d), BF16),
        ],
        limit=16,
    )
    shift = lambda v, k: lax.ppermute(v, "wide", [(i, i ^ k) for i in around])
    x_rows = shift(pay, 1)
    known, rich = call(
        functools.partial(pair_kernel, halo), (pay, x_rows, base_c),
        [((4 * COARSE_DEV, d), BF16), ((4 * COARSE_DEV + 2 * halo, d), BF16)], limit=1,
    )
    (base_f,) = call(
        base_kernel,
        (oh1, table, edge_weight_in, e_bias, fine_edges, edge_weight_out, node_weight_out),
        [((edges, d), F32)],
        limit=16,
    )
    ready, hidden, part, pick = call(
        prep_kernel, (partner, x_rows, base_f, base_c, oh2, sel, pack, edge_weight_in),
        [
            ((table_b, d), BF16),
            ((edges, d), BF16),
            ((LATE + coarse_count, d), F32),
            ((LATE + coarse_count, LANES + sel.shape[1]), BF16),
        ],
        limit=12,
    )
    if n_patches == RING:
        spot = lambda p, c: p % n_patches * 2 + c
        split = lambda v, steps: lax.ppermute(
            v, ("wide", "narrow"),
            [(spot(p, c), spot(steps[c](p), c)) for p in around for c in range(2)],
        )
        first = split(rich, (lambda p: p + 2, lambda p: p - 2))
        second = split(known, (lambda p: p ^ 1, lambda p: p + 4))
        (both,) = call(
            both_kernel, (first, second, base_f, ready), [((8 * COARSE_DEV + 2 * halo, d), BF16)], limit=1
        )
        other = lax.ppermute(both, "narrow", [(0, 1), (1, 0)])
        far, picks = call(
            functools.partial(collect_kernel, halo), (known, both, other),
            [((2 * block, d), BF16), ((16 * COARSE_DEV, d), BF16)], limit=1,
        )
        pieces = (picks,)
    else:
        y_rows = lax.ppermute(
            pay, "wide", [(i, (i - 1 if i % 2 == 0 else i + 1) % n_patches) for i in around]
        )
        (far,) = call(
            functools.partial(wrap_kernel, halo), (y_rows,), [((2 * block, d), BF16)], limit=1
        )
        have = 2
        while True:
            pieces = [known]
            for k in range(1, min(4, n_patches // have)):
                pieces.append(shift(known, k * have))
            have *= len(pieces)
            if have == n_patches:
                break
            (known,) = call(
                join_kernel, pieces, [((len(pieces) * known.shape[0], d), BF16)], limit=2
            )
    coarse_rows = sum(p.shape[0] for p in pieces)

    (total,) = call(
        early_kernel, (hidden, inc_e, edge_weight_out), [((nodes, d), F32)],
        scratch=[pltpu.VMEM((edges, d), BF16)], limit=12,
    )
    (out,) = call(
        functools.partial(last_kernel, len(pieces)),
        (ready, far, nl, base_f, part, pick, oh2, inc_f, inc_l, late, total,
         shifts, nu, edge_weight_in, edge_weight_out, node_weight_in, node_weight_out,
         e_gain, n_gain, n_shift, *pieces),
        [((nodes, d), BF16)],
        scratch=[
            pltpu.VMEM((LANES + coarse_rows, d), BF16),
            pltpu.VMEM((table_b, d), BF16),
            pltpu.VMEM((edges, d), BF16),
            pltpu.VMEM((edges, d), BF16),
            pltpu.VMEM((nodes, d), F32),
        ],
        limit=16,
        far_out=True,
    )
    return out


def solution(mesh):
    axes = ("grp", "wide", "narrow")
    matrix, vector, whole = P(axes, None), P(axes), P()
    return jax.shard_map(
        shards,
        mesh=mesh,
        in_specs=(matrix, matrix, vector, vector, matrix, vector, vector) + (whole,) * 10,
        out_specs=matrix,
        check_vma=False,
    )
```

profile of v0, /device:TPU:0, one launch (start us, length us, event | category | flops | bytes accessed | tf_op | source)
XLA Modules:
  0.0 16.6 jit_solution(13673573698561685866)
XLA Ops:
  0.0 0.5 %collective-permute-start = (bf16[160,512]{1,0:T(8,128)(2,1)}, bf16[160,512]{1,0:T(8,128)(2,1)S(1)}, u32[]{:S(2)}, u32[]{:S(2)}) collective-permute-start(bf16[160,512]{1,0:T(8,128)(2,1)} %refs_0_.1), channel_id=1, source_target_pairs={{0,1},{1,0},{2,3},{3,2},{4,5},{5,4},{6,7},{7,6},{8,9},{9,8},{10,11... | collective-permute-start | bytes 491528 | tf_op jit(solution)/shard_map/ppermute | solution.py:311
  0.5 1.2 %shard_map.163 = (bf16[160,512]{1,0:T(8,128)(2,1)S(1)}, s32[1,960]{1,0:T(1,128)S(1)}, s32[1,960]{1,0:T(1,128)S(1)}, s32[1,32]{1,0:T(1,128)S(1)}, s32[1,32]{1,0:T...) custom-call(bf16[160,512]{1,0:T(8,128)(2,1)} %refs_0_.1, ...), custom_call_target="tpu_custom_call" | custom-call | tf_op jit(solution)/shard_map/pallas_call | solution.py:281
  1.7 0.0 copy-start.2
  1.7 0.0 copy-start.3
  1.7 0.0 copy-start.4
  1.7 0.0 collective-permute-done.partner
  1.8 2.9 %collective-permute-start.1 = (bf16[48,512]{1,0:T(8,128)(2,1)S(1)}, bf16[48,512]{1,0:T(8,128)(2,1)S(1)}, u32[]{:S(2)}, u32[]{:S(2)}) collective-permute-start(bf16[48,512]{1,0:T(8,128)(2,1)S(1)} %shard_map.164.pay), channel_id=1, source_target_pairs={{0,2},{2,0},{4,6},{6,4},{8,10},{10,8},{12,14},{14,12},{1,3},{3,1},... | collective-permute-start | bytes 147464 | tf_op jit(solution)/shard_map/ppermute | solution.py:339
  4.7 0.0 copy-done
  4.7 0.0 copy-done.1
  4.7 0.0 copy-done.5
  4.7 1.3 %shard_map.165 = (f32[32,512]{1,0:T(8,128)S(1)}, bf16[960,384]{1,0:T(8,128)(2,1)S(1)}, bf16[960,256]{1,0:T(8,128)(2,1)S(1)}, bf16[32,64]{1,0:T(8,128)(2,1)S(1)},...) custom-call(bf16[160,512]{1,0:T(8,128)(2,1)S(1)} %get-tuple-element., ...), custom_call_target="tpu_custom_call" | custom-call | tf_op jit(solution)/shard_map/pallas_call | solution.py:281
  5.9 0.8 %collective-permute-done.1.x_rows = bf16[48,512]{1,0:T(8,128)(2,1)S(1)} collective-permute-done((bf16[48,512]{1,0:T(8,128)(2,1)S(1)}, bf16[48,512]{1,0:T(8,128)(2,1)S(1)}, u32[]{:S(2)}, u32[]{:S(2)}) %collective-permute-start.1) | collective-permute-done | bytes 49184 | tf_op jit(solution)/shard_map/ppermute | solution.py:339
  6.7 2.2 %collective-permute-start.2 = (bf16[56,512]{1,0:T(8,128)(2,1)S(1)}, bf16[56,512]{1,0:T(8,128)(2,1)S(1)}, u32[]{:S(2)}, u32[]{:S(2)}) collective-permute-start(bf16[56,512]{1,0:T(8,128)(2,1)S(1)} %get-tuple-element.52), channel_id=1, source_target_pairs={{0,4},{1,13},{2,6},{3,15},{4,8},{5,1},{6,10},{7,3},{8,12},{9,5},{1... | collective-permute-start | bytes 172040 | tf_op jit(solution)/shard_map/ppermute | solution.py:363
  8.9 1.5 %collective-permute-start.3 = (bf16[16,512]{1,0:T(8,128)(2,1)S(1)}, bf16[16,512]{1,0:T(8,128)(2,1)S(1)}, u32[]{:S(2)}, u32[]{:S(2)}) collective-permute-start(bf16[16,512]{1,0:T(8,128)(2,1)S(1)} %get-tuple-element.51.known), channel_id=1, source_target_pairs={{0,2},{1,9},{2,0},{3,11},{4,6},{5,13},{6,4},{7,15},{8,10},{9,1},{1... | collective-permute-start | bytes 49160 | tf_op jit(solution)/shard_map/ppermute | solution.py:363
  10.4 0.0 copy-done.2
  10.4 0.0 copy-done.3
  10.4 1.2 %shard_map.166.base_f._ = f32[960,512]{1,0:T(8,128)S(1)} custom-call(bf16[960,384]{1,0:T(8,128)(2,1)S(1)} %get-tuple-element.44.oh1, bf16[384,512]{1,0:T(8,128)(2,1)S(1)} %get-tuple-element.45.table, bf16[1536,512]{1,0:T(8,128)(2,1)S(1)} %copy-done, f32[1,512]{1,0:T(1,128)S(1)} %get-tuple-element.41.e_bias, bf16[960,512]{1,0:T(8,128)(2,1)S(1)} %copy-done.3, ...), custom_call_target="tpu_custom_call" | custom-call | tf_op jit(solution)/shard_map/pallas_call | solution.py:281
  11.6 1.3 %shard_map.167 = (bf16[256,512]{1,0:T(8,128)(2,1)S(1)}, bf16[960,512]{1,0:T(8,128)(2,1)S(1)}, f32[160,512]{1,0:T(8,128)S(1)}, bf16[160,192]{1,0:T(8,128)(2,1)S(1)}) custom-call(bf16[160,512]{1,0:T(8,128)(2,1)S(1)} %collective-permute-done.partner, bf16[48,512]{1,0:T(8,128)(2,1)S(1)} %collective-permute-done.1.x_rows, f32[960,512]{1,0:T(8,128)S(1)} %shard_map.166.base_f._, ...), custom_call_target="tpu_custom_call" | custom-call | tf_op jit(solution)/shard_map/pallas_call | solution.py:281
  12.9 0.0 collective-permute-done.3.second
  12.9 0.2 %collective-permute-done.2.first = bf16[56,512]{1,0:T(8,128)(2,1)S(1)} collective-permute-done((bf16[56,512]{1,0:T(8,128)(2,1)S(1)}, bf16[56,512]{1,0:T(8,128)(2,1)S(1)}, u32[]{:S(2)}, u32[]{:S(2)}) %collective-permute-start.2) | collective-permute-done | bytes 57376 | tf_op jit(solution)/shard_map/ppermute | solution.py:363
  13.1 0.2 %collective-permute-start.4 = (bf16[72,512]{1,0:T(8,128)(2,1)S(1)}, bf16[72,512]{1,0:T(8,128)(2,1)S(1)}, u32[]{:S(2)}, u32[]{:S(2)}) collective-permute-start(bf16[72,512]{1,0:T(8,128)(2,1)S(1)} %shard_map.169.both), channel_id=1, source_target_pairs={{0,1},{1,0},{2,3},{3,2},{4,5},{5,4},{6,7},{7,6},{8,9},{9,8},{10,11... | collective-permute-start | bytes 221192 | tf_op jit(solution)/shard_map/ppermute | solution.py:372
  13.3 1.0 %shard_map.171.total = f32[160,512]{1,0:T(8,128)S(1)} custom-call(bf16[960,512]{1,0:T(8,128)(2,1)S(1)} %get-tuple-element.59.hidden, bf16[160,960]{1,0:T(8,128)(2,1)S(1)} %get-tuple-element.60.inc_e, bf16[512,512]{1,0:T(8,128)(2,1)S(1)} %copy-done.2), custom_call_target="tpu_custom_call" | custom-call | tf_op jit(solution)/shard_map/pallas_call | solution.py:281
  14.3 0.0 collective-permute-done.4.other
  14.4 2.2 %shard_map.172 = bf16[160,512]{1,0:T(8,128)(2,1)} custom-call(bf16[256,512]{1,0:T(8,128)(2,1)S(1)} %get-tuple-element.50.__.ready, bf16[48,512]{1,0:T(8,128)(2,1)S(1)} %get-tuple-element.53.far, bf16[160,512]{1,0:T(8,128)(2,1)S(1)} %get-tuple-element.36.nl, f32[960,512]{1,0:T(8,128)S(1)} %shard_map.166.base_f._, f32[160,512]{1,0:T(8,128)S(1)} %get-tuple-element.54.part, ...), custom_call_target="tpu_custom_call" | custom-call | tf_op jit(solution)/shard_map/pallas_call | solution.py:281
  (8 shorter events, 0.1 us)
Async XLA Ops:
  0.0 1.7 %collective-permute-start = (bf16[160,512]{1,0:T(8,128)(2,1)}, bf16[160,512]{1,0:T(8,128)(2,1)S(1)}, u32[]{:S(2)}, u32[]{:S(2)}) collective-permute-start(bf16[160,512]{1,0:T(8,128)(2,1)} %refs_0_.1), channel_id=1, source_target_pairs={{0,1},{1,0},{2,3},{3,2},{4,5},{5,4},{6,7},{7,6},{8,9},{9,8},{10,11... | collective-permute-start | bytes 491528 | tf_op jit(solution)/shard_map/ppermute | solution.py:311
  0.5 4.2 %copy-start = (bf16[1536,512]{1,0:T(8,128)(2,1)S(1)}, bf16[1536,512]{1,0:T(8,128)(2,1)}, u32[]{:S(2)}) copy-start(bf16[1536,512]{1,0:T(8,128)(2,1)} %w_in.7) | copy-start | bytes 4718596
  0.5 4.2 %copy-start.1 = (bf16[1024,512]{1,0:T(8,128)(2,1)S(1)}, bf16[1024,512]{1,0:T(8,128)(2,1)}, u32[]{:S(2)}) copy-start(bf16[1024,512]{1,0:T(8,128)(2,1)} %u_in.3) | copy-start | bytes 3145732
  0.5 4.2 %copy-start.5 = (bf16[32,512]{1,0:T(8,128)(2,1)S(1)}, bf16[32,512]{1,0:T(8,128)(2,1)}, u32[]{:S(2)}) copy-start(bf16[32,512]{1,0:T(8,128)(2,1)} %ce.1) | copy-start | bytes 98308
  1.7 8.7 %copy-start.2 = (bf16[512,512]{1,0:T(8,128)(2,1)S(1)}, bf16[512,512]{1,0:T(8,128)(2,1)}, u32[]{:S(2)}) copy-start(bf16[512,512]{1,0:T(8,128)(2,1)} %w_out.3) | copy-start | bytes 1572868
  1.7 8.7 %copy-start.3 = (bf16[960,512]{1,0:T(8,128)(2,1)S(1)}, bf16[960,512]{1,0:T(8,128)(2,1)}, u32[]{:S(2)}) copy-start(bf16[960,512]{1,0:T(8,128)(2,1)} %fe.1) | copy-start | bytes 2949124
  1.7 8.7 %copy-start.4 = (bf16[512,512]{1,0:T(8,128)(2,1)S(1)}, bf16[512,512]{1,0:T(8,128)(2,1)}, u32[]{:S(2)}) copy-start(bf16[512,512]{1,0:T(8,128)(2,1)} %u_out.1) | copy-start | bytes 1572868
  1.8 5.0 %collective-permute-start.1 = (bf16[48,512]{1,0:T(8,128)(2,1)S(1)}, bf16[48,512]{1,0:T(8,128)(2,1)S(1)}, u32[]{:S(2)}, u32[]{:S(2)}) collective-permute-start(bf16[48,512]{1,0:T(8,128)(2,1)S(1)} %shard_map.164.pay), channel_id=1, source_target_pairs={{0,2},{2,0},{4,6},{6,4},{8,10},{10,8},{12,14},{14,12},{1,3},{3,1},... | collective-permute-start | bytes 147464 | tf_op jit(solution)/shard_map/ppermute | solution.py:339
  6.7 6.3 %collective-permute-start.2 = (bf16[56,512]{1,0:T(8,128)(2,1)S(1)}, bf16[56,512]{1,0:T(8,128)(2,1)S(1)}, u32[]{:S(2)}, u32[]{:S(2)}) collective-permute-start(bf16[56,512]{1,0:T(8,128)(2,1)S(1)} %get-tuple-element.52), channel_id=1, source_target_pairs={{0,4},{1,13},{2,6},{3,15},{4,8},{5,1},{6,10},{7,3},{8,12},{9,5},{1... | collective-permute-start | bytes 172040 | tf_op jit(solution)/shard_map/ppermute | solution.py:363
  8.9 4.0 %collective-permute-start.3 = (bf16[16,512]{1,0:T(8,128)(2,1)S(1)}, bf16[16,512]{1,0:T(8,128)(2,1)S(1)}, u32[]{:S(2)}, u32[]{:S(2)}) collective-permute-start(bf16[16,512]{1,0:T(8,128)(2,1)S(1)} %get-tuple-element.51.known), channel_id=1, source_target_pairs={{0,2},{1,9},{2,0},{3,11},{4,6},{5,13},{6,4},{7,15},{8,10},{9,1},{1... | collective-permute-start | bytes 49160 | tf_op jit(solution)/shard_map/ppermute | solution.py:363
  13.1 1.3 %collective-permute-start.4 = (bf16[72,512]{1,0:T(8,128)(2,1)S(1)}, bf16[72,512]{1,0:T(8,128)(2,1)S(1)}, u32[]{:S(2)}, u32[]{:S(2)}) collective-permute-start(bf16[72,512]{1,0:T(8,128)(2,1)S(1)} %shard_map.169.both), channel_id=1, source_target_pairs={{0,1},{1,0},{2,3},{3,2},{4,5},{5,4},{6,7},{7,6},{8,9},{9,8},{10,11... | collective-permute-start | bytes 221192 | tf_op jit(solution)/shard_map/ppermute | solution.py:372
where the time goes:
time: 16.8 us; the launch traced here: 16.6 us
  Pallas kernels  8.25 us (49%)
  starting transfers between devices  7.23 us (43%)
  waiting for transfers between devices  1.03 us (6%)
    pallas_call x10, Pallas kernels, call(): pl.pallas_call(kernel, out_shape=tuple((kind(*o) for o in outs)), in_spec...  8.25 us
    ppermute x2, starting transfers between devices, shards(): lax.ppermute(v, ('wide', 'narrow'), [(spot(p, c), spot(steps[c](p), c)) f...  3.65 us
    ppermute x1, starting transfers between devices, shards(): shift = lambda v, k: lax.ppermute(v, 'wide', [(i, i ^ k) for i in around])  2.9 us
    ppermute x1, waiting for transfers between devices, shards(): shift = lambda v, k: lax.ppermute(v, 'wide', [(i, i ^ k) for i in around])  0.8 us
    ppermute x1, starting transfers between devices, shards(): partner = lax.ppermute(node_latent, 'narrow', [(0, 1), (1, 0)])  0.49 us
  transfers between devices with their start and end apart: 5, of which 2 were waited for; matrix products, arithmetic and copies ran while one was open for 0% of the time, Pallas kernels for 36%

commit v1 on v0

--- a/solution.py
+++ b/solution.py
@@ -170,8 +170,7 @@
     chosen = lax.broadcasted_iota(jnp.int32, pack.shape, 0) == rank
     chosen = jnp.where(chosen, 1.0, 0.0).astype(BF16)
     pack[...] = chosen
-    over = jnp.sum(late_row, axis=1, keepdims=True) > LATE
-    late[...] = jnp.broadcast_to(jnp.where(over, 1.0, 0.0), late.shape)
+    late[...] = late_row
     marks, marks_c = incidence(recv), incidence(recv_c)
     inc_f[...] = marks.astype(BF16)
     inc_e[...] = (marks * (1.0 - late_row)).astype(BF16)
@@ -217,7 +216,7 @@
     coarse_bits = half.astype(BF16)
     fine_bits = (half - coarse_bits.astype(F32)).astype(BF16)
     late = pack.shape[0]
-    part[:late, :] = dot(pack[...], coarse_bits) + dot(pack[...], fine_bits)
+    part[:late, :] = dot(pack[...], coarse_bits)
     part[late:, :] = base_c[...]
     pick[...] = jnp.zeros_like(pick)
     pick[:late, :LANES] = dot(pack[...], oh2[:, oh2.shape[1] - LANES :]).astype(BF16)
@@ -248,7 +247,7 @@
     some = normalized(dot(silu_of_half(half).astype(BF16), w_out[...])).astype(BF16)
     acc[...] = total[...] + dot(inc_l[...], some)
 
-    @pl.when(late[0, 0] > 0)
+    @pl.when(jnp.sum(late[...]) > LATE)
     def _():
         a = ready.shape[0] - far.shape[0]
         table[:a, :] = ready[:a, :]
@@ -329,7 +328,7 @@
             ((nodes, edges), BF16),
             ((nodes, LATE + coarse_count), BF16),
             ((LATE, edges), BF16),
-            ((8, LANES), F32),
+            ((1, edges), F32),
             ((nodes, d), F32),
             ((nodes, d), F32),
             ((table_a, d), BF16),

time: 16.8 us -> 16.8 us (level)
  Pallas kernels: 8.25 us -> 8.01 us
  waiting for transfers between devices: 1.03 us -> 1.27 us
    ppermute x2, waiting for transfers between devices: 0.19 us -> 0.43 us  [shards(): lax.ppermute(v, ('wide', 'narrow'), [(spot(p, c), spot(steps[c](p), c)) f...]
    pallas_call x10, Pallas kernels: 8.25 us -> 8.01 us  [call(): pl.pallas_call(kernel, out_shape=tuple((kind(*o) for o in outs)), in_spec...]
  transfers between devices with their start and end apart: 5 -> 5, of which waited for: 2 -> 2; matrix products, arithmetic and copies ran while one was open for 0% -> 0% of each run, Pallas kernels for 36% -> 34%
where the time goes in v1:
time: 16.8 us; the launch traced here: 16.6 us
  Pallas kernels  8.01 us (48%)
  starting transfers between devices  7.23 us (43%)
  waiting for transfers between devices  1.27 us (8%)
    pallas_call x10, Pallas kernels, call(): pl.pallas_call(kernel, out_shape=tuple((kind(*o) for o in outs)), in_spec...  8.01 us
    ppermute x2, starting transfers between devices, shards(): lax.ppermute(v, ('wide', 'narrow'), [(spot(p, c), spot(steps[c](p), c)) f...  3.65 us
    ppermute x1, starting transfers between devices, shards(): shift = lambda v, k: lax.ppermute(v, 'wide', [(i, i ^ k) for i in around])  2.9 us
    ppermute x1, waiting for transfers between devices, shards(): shift = lambda v, k: lax.ppermute(v, 'wide', [(i, i ^ k) for i in around])  0.8 us
    ppermute x1, starting transfers between devices, shards(): partner = lax.ppermute(node_latent, 'narrow', [(0, 1), (1, 0)])  0.49 us
    ppermute x2, waiting for transfers between devices, shards(): lax.ppermute(v, ('wide', 'narrow'), [(spot(p, c), spot(steps[c](p), c)) f...  0.43 us
  transfers between devices with their start and end apart: 5, of which 2 were waited for; matrix products, arithmetic and copies ran while one was open for 0% of the time, Pallas kernels for 34%

profile of v1, /device:TPU:0, one launch (start us, length us, event | category | flops | bytes accessed | tf_op | source)
XLA Modules:
  0.0 16.6 jit_solution(222385994429305334)
XLA Ops:
  0.0 0.5 %collective-permute-start = (bf16[160,512]{1,0:T(8,128)(2,1)}, bf16[160,512]{1,0:T(8,128)(2,1)S(1)}, u32[]{:S(2)}, u32[]{:S(2)}) collective-permute-start(bf16[160,512]{1,0:T(8,128)(2,1)} %refs_0_.1), channel_id=1, source_target_pairs={{0,1},{1,0},{2,3},{3,2},{4,5},{5,4},{6,7},{7,6},{8,9},{9,8},{10,11... | collective-permute-start | bytes 491528 | tf_op jit(solution)/shard_map/ppermute | solution.py:310
  0.5 1.2 %shard_map.163 = (bf16[160,512]{1,0:T(8,128)(2,1)S(1)}, s32[1,960]{1,0:T(1,128)S(1)}, s32[1,960]{1,0:T(1,128)S(1)}, s32[1,32]{1,0:T(1,128)S(1)}, s32[1,32]{1,0:T...) custom-call(bf16[160,512]{1,0:T(8,128)(2,1)} %refs_0_.1, ...), custom_call_target="tpu_custom_call" | custom-call | tf_op jit(solution)/shard_map/pallas_call | solution.py:280
  1.7 0.0 copy-start.2
  1.7 0.0 copy-start.3
  1.7 0.0 copy-start.4
  1.7 0.0 collective-permute-done.partner
  1.8 2.9 %collective-permute-start.1 = (bf16[48,512]{1,0:T(8,128)(2,1)S(1)}, bf16[48,512]{1,0:T(8,128)(2,1)S(1)}, u32[]{:S(2)}, u32[]{:S(2)}) collective-permute-start(bf16[48,512]{1,0:T(8,128)(2,1)S(1)} %shard_map.164.pay), channel_id=1, source_target_pairs={{0,2},{2,0},{4,6},{6,4},{8,10},{10,8},{12,14},{14,12},{1,3},{3,1},... | collective-permute-start | bytes 147464 | tf_op jit(solution)/shard_map/ppermute | solution.py:338
  4.7 0.0 copy-done
  4.7 0.0 copy-done.1
  4.7 0.0 copy-done.5
  4.7 1.3 %shard_map.165 = (f32[32,512]{1,0:T(8,128)S(1)}, bf16[960,384]{1,0:T(8,128)(2,1)S(1)}, bf16[960,256]{1,0:T(8,128)(2,1)S(1)}, bf16[32,64]{1,0:T(8,128)(2,1)S(1)},...) custom-call(bf16[160,512]{1,0:T(8,128)(2,1)S(1)} %get-tuple-element., ...), custom_call_target="tpu_custom_call" | custom-call | tf_op jit(solution)/shard_map/pallas_call | solution.py:280
  5.9 0.8 %collective-permute-done.1.x_rows = bf16[48,512]{1,0:T(8,128)(2,1)S(1)} collective-permute-done((bf16[48,512]{1,0:T(8,128)(2,1)S(1)}, bf16[48,512]{1,0:T(8,128)(2,1)S(1)}, u32[]{:S(2)}, u32[]{:S(2)}) %collective-permute-start.1) | collective-permute-done | bytes 49184 | tf_op jit(solution)/shard_map/ppermute | solution.py:338
  6.7 2.2 %collective-permute-start.2 = (bf16[56,512]{1,0:T(8,128)(2,1)S(1)}, bf16[56,512]{1,0:T(8,128)(2,1)S(1)}, u32[]{:S(2)}, u32[]{:S(2)}) collective-permute-start(bf16[56,512]{1,0:T(8,128)(2,1)S(1)} %get-tuple-element.52), channel_id=1, source_target_pairs={{0,4},{1,13},{2,6},{3,15},{4,8},{5,1},{6,10},{7,3},{8,12},{9,5},{1... | collective-permute-start | bytes 172040 | tf_op jit(solution)/shard_map/ppermute | solution.py:362
  8.9 1.5 %collective-permute-start.3 = (bf16[16,512]{1,0:T(8,128)(2,1)S(1)}, bf16[16,512]{1,0:T(8,128)(2,1)S(1)}, u32[]{:S(2)}, u32[]{:S(2)}) collective-permute-start(bf16[16,512]{1,0:T(8,128)(2,1)S(1)} %get-tuple-element.51.known), channel_id=1, source_target_pairs={{0,2},{1,9},{2,0},{3,11},{4,6},{5,13},{6,4},{7,15},{8,10},{9,1},{1... | collective-permute-start | bytes 49160 | tf_op jit(solution)/shard_map/ppermute | solution.py:362
  10.4 0.0 copy-done.2
  10.4 0.0 copy-done.3
  10.4 1.2 %shard_map.166.base_f._ = f32[960,512]{1,0:T(8,128)S(1)} custom-call(bf16[960,384]{1,0:T(8,128)(2,1)S(1)} %get-tuple-element.44.oh1, bf16[384,512]{1,0:T(8,128)(2,1)S(1)} %get-tuple-element.45.table, bf16[1536,512]{1,0:T(8,128)(2,1)S(1)} %copy-done, f32[1,512]{1,0:T(1,128)S(1)} %get-tuple-element.41.e_bias, bf16[960,512]{1,0:T(8,128)(2,1)S(1)} %copy-done.3, ...), custom_call_target="tpu_custom_call" | custom-call | tf_op jit(solution)/shard_map/pallas_call | solution.py:280
  11.6 1.1 %shard_map.167 = (bf16[256,512]{1,0:T(8,128)(2,1)S(1)}, bf16[960,512]{1,0:T(8,128)(2,1)S(1)}, f32[160,512]{1,0:T(8,128)S(1)}, bf16[160,192]{1,0:T(8,128)(2,1)S(1)}) custom-call(bf16[160,512]{1,0:T(8,128)(2,1)S(1)} %collective-permute-done.partner, bf16[48,512]{1,0:T(8,128)(2,1)S(1)} %collective-permute-done.1.x_rows, f32[960,512]{1,0:T(8,128)S(1)} %shard_map.166.base_f._, ...), custom_call_target="tpu_custom_call" | custom-call | tf_op jit(solution)/shard_map/pallas_call | solution.py:280
  12.6 0.0 collective-permute-done.3.second
  12.7 0.4 %collective-permute-done.2.first = bf16[56,512]{1,0:T(8,128)(2,1)S(1)} collective-permute-done((bf16[56,512]{1,0:T(8,128)(2,1)S(1)}, bf16[56,512]{1,0:T(8,128)(2,1)S(1)}, u32[]{:S(2)}, u32[]{:S(2)}) %collective-permute-start.2) | collective-permute-done | bytes 57376 | tf_op jit(solution)/shard_map/ppermute | solution.py:362
  13.1 0.2 %collective-permute-start.4 = (bf16[72,512]{1,0:T(8,128)(2,1)S(1)}, bf16[72,512]{1,0:T(8,128)(2,1)S(1)}, u32[]{:S(2)}, u32[]{:S(2)}) collective-permute-start(bf16[72,512]{1,0:T(8,128)(2,1)S(1)} %shard_map.169.both), channel_id=1, source_target_pairs={{0,1},{1,0},{2,3},{3,2},{4,5},{5,4},{6,7},{7,6},{8,9},{9,8},{10,11... | collective-permute-start | bytes 221192 | tf_op jit(solution)/shard_map/ppermute | solution.py:371
  13.3 1.0 %shard_map.171.total = f32[160,512]{1,0:T(8,128)S(1)} custom-call(bf16[960,512]{1,0:T(8,128)(2,1)S(1)} %get-tuple-element.59.hidden, bf16[160,960]{1,0:T(8,128)(2,1)S(1)} %get-tuple-element.60.inc_e, bf16[512,512]{1,0:T(8,128)(2,1)S(1)} %copy-done.2), custom_call_target="tpu_custom_call" | custom-call | tf_op jit(solution)/shard_map/pallas_call | solution.py:280
  14.3 0.0 collective-permute-done.4.other
  14.4 2.2 %shard_map.172 = bf16[160,512]{1,0:T(8,128)(2,1)} custom-call(bf16[256,512]{1,0:T(8,128)(2,1)S(1)} %get-tuple-element.50.__.ready, bf16[48,512]{1,0:T(8,128)(2,1)S(1)} %get-tuple-element.53.far, bf16[160,512]{1,0:T(8,128)(2,1)S(1)} %get-tuple-element.36.nl, f32[960,512]{1,0:T(8,128)S(1)} %shard_map.166.base_f._, f32[160,512]{1,0:T(8,128)S(1)} %get-tuple-element.54.part, ...), custom_call_target="tpu_custom_call" | custom-call | tf_op jit(solution)/shard_map/pallas_call | solution.py:280
  (8 shorter events, 0.1 us)
Async XLA Ops:
  0.0 1.7 %collective-permute-start = (bf16[160,512]{1,0:T(8,128)(2,1)}, bf16[160,512]{1,0:T(8,128)(2,1)S(1)}, u32[]{:S(2)}, u32[]{:S(2)}) collective-permute-start(bf16[160,512]{1,0:T(8,128)(2,1)} %refs_0_.1), channel_id=1, source_target_pairs={{0,1},{1,0},{2,3},{3,2},{4,5},{5,4},{6,7},{7,6},{8,9},{9,8},{10,11... | collective-permute-start | bytes 491528 | tf_op jit(solution)/shard_map/ppermute | solution.py:310
  0.5 4.2 %copy-start = (bf16[1536,512]{1,0:T(8,128)(2,1)S(1)}, bf16[1536,512]{1,0:T(8,128)(2,1)}, u32[]{:S(2)}) copy-start(bf16[1536,512]{1,0:T(8,128)(2,1)} %w_in.7) | copy-start | bytes 4718596
  0.5 4.2 %copy-start.1 = (bf16[1024,512]{1,0:T(8,128)(2,1)S(1)}, bf16[1024,512]{1,0:T(8,128)(2,1)}, u32[]{:S(2)}) copy-start(bf16[1024,512]{1,0:T(8,128)(2,1)} %u_in.3) | copy-start | bytes 3145732
  0.5 4.2 %copy-start.5 = (bf16[32,512]{1,0:T(8,128)(2,1)S(1)}, bf16[32,512]{1,0:T(8,128)(2,1)}, u32[]{:S(2)}) copy-start(bf16[32,512]{1,0:T(8,128)(2,1)} %ce.1) | copy-start | bytes 98308
  1.7 8.7 %copy-start.2 = (bf16[512,512]{1,0:T(8,128)(2,1)S(1)}, bf16[512,512]{1,0:T(8,128)(2,1)}, u32[]{:S(2)}) copy-start(bf16[512,512]{1,0:T(8,128)(2,1)} %w_out.3) | copy-start | bytes 1572868
  1.7 8.7 %copy-start.3 = (bf16[960,512]{1,0:T(8,128)(2,1)S(1)}, bf16[960,512]{1,0:T(8,128)(2,1)}, u32[]{:S(2)}) copy-start(bf16[960,512]{1,0:T(8,128)(2,1)} %fe.1) | copy-start | bytes 2949124
  1.7 8.7 %copy-start.4 = (bf16[512,512]{1,0:T(8,128)(2,1)S(1)}, bf16[512,512]{1,0:T(8,128)(2,1)}, u32[]{:S(2)}) copy-start(bf16[512,512]{1,0:T(8,128)(2,1)} %u_out.1) | copy-start | bytes 1572868
  1.8 5.0 %collective-permute-start.1 = (bf16[48,512]{1,0:T(8,128)(2,1)S(1)}, bf16[48,512]{1,0:T(8,128)(2,1)S(1)}, u32[]{:S(2)}, u32[]{:S(2)}) collective-permute-start(bf16[48,512]{1,0:T(8,128)(2,1)S(1)} %shard_map.164.pay), channel_id=1, source_target_pairs={{0,2},{2,0},{4,6},{6,4},{8,10},{10,8},{12,14},{14,12},{1,3},{3,1},... | collective-permute-start | bytes 147464 | tf_op jit(solution)/shard_map/ppermute | solution.py:338
  6.7 6.3 %collective-permute-start.2 = (bf16[56,512]{1,0:T(8,128)(2,1)S(1)}, bf16[56,512]{1,0:T(8,128)(2,1)S(1)}, u32[]{:S(2)}, u32[]{:S(2)}) collective-permute-start(bf16[56,512]{1,0:T(8,128)(2,1)S(1)} %get-tuple-element.52), channel_id=1, source_target_pairs={{0,4},{1,13},{2,6},{3,15},{4,8},{5,1},{6,10},{7,3},{8,12},{9,5},{1... | collective-permute-start | bytes 172040 | tf_op jit(solution)/shard_map/ppermute | solution.py:362
  8.9 3.7 %collective-permute-start.3 = (bf16[16,512]{1,0:T(8,128)(2,1)S(1)}, bf16[16,512]{1,0:T(8,128)(2,1)S(1)}, u32[]{:S(2)}, u32[]{:S(2)}) collective-permute-start(bf16[16,512]{1,0:T(8,128)(2,1)S(1)} %get-tuple-element.51.known), channel_id=1, source_target_pairs={{0,2},{1,9},{2,0},{3,11},{4,6},{5,13},{6,4},{7,15},{8,10},{9,1},{1... | collective-permute-start | bytes 49160 | tf_op jit(solution)/shard_map/ppermute | solution.py:362
  13.1 1.3 %collective-permute-start.4 = (bf16[72,512]{1,0:T(8,128)(2,1)S(1)}, bf16[72,512]{1,0:T(8,128)(2,1)S(1)}, u32[]{:S(2)}, u32[]{:S(2)}) collective-permute-start(bf16[72,512]{1,0:T(8,128)(2,1)S(1)} %shard_map.169.both), channel_id=1, source_target_pairs={{0,1},{1,0},{2,3},{3,2},{4,5},{5,4},{6,7},{7,6},{8,9},{9,8},{10,11... | collective-permute-start | bytes 221192 | tf_op jit(solution)/shard_map/ppermute | solution.py:371
